TPU v7x, 32 devices: a whole 2x2x4 slice. The times are simulated.
32 devices in a mesh: ch: 4 (over z), ha: 2 (over x), dp: 4 (over y, core).
Axes of the slice: x: 2, y: 2, z: 4, core: 2. Of those that a mesh axis runs over, the one named last changes fastest.
Arguments:
- features: bfloat16 [384, 4, 4, 4, 128], P('ch', 'dp', None, 'ha'), may hold values from -26 to 26
- frame_count: int32 [4], P('dp'), may hold values from 1 to 4, as said below
- norm1_gain: float32 [384], P('ch'), may hold values from 0.5 to 2
- norm1_shift: float32 [384], P('ch'), may hold values from -3 to 3
- qkv_weight: bfloat16 [384, 1152], replicated, may hold values from -0.51031036 to 0.51031036
- qkv_bias: float32 [1152], replicated, may hold values from -3 to 3
- out_weight: bfloat16 [384, 384], replicated, may hold values from -0.3125 to 0.3125
- out_bias: float32 [384], replicated, may hold values from -3 to 3
- norm2_gain: float32 [384], P('ch'), may hold values from 0.5 to 2
- norm2_shift: float32 [384], P('ch'), may hold values from -3 to 3
- conv_weight: bfloat16 [3, 3, 3, 384, 384], P(None, None, None, 'ch'), may hold values from -0.0625 to 0.0625
- conv_bias: float32 [384], P('ch'), may hold values from -3 to 3
- cotangent: bfloat16 [384, 4, 4, 4, 128], P('ch', 'dp', None, 'ha'), may hold values from -0.0625 to 0.0625
Outputs:
- mixed: bfloat16 [384, 4, 4, 4, 128], P('ch', 'dp', None, 'ha')
- weight_grad: float32 [3, 3, 3, 384, 384], P(None, None, None, 'ch')
Inputs may be any that keep to these rules, and one draw needn't show every extreme that they name: `frame_count`: some clip has all 4 frames valid and some clip only one.
All inputs are finite; a program needn't handle non-finite values.
Results may differ from a plain program's by a relative error of at most 0.015.
Values may be sent and summed in bfloat16 or wider, within the bound.
A program may use at most 64 MiB of HBM per device.

v0:
```python
import jax
import jax.numpy as jnp
from jax import lax
from jax.sharding import PartitionSpec as P

GROUPS = 32
EPS = 1e-06


def padded_2(x, sides, width):
    for axis, dim in sides:
        count, length = (lax.axis_size(axis), x.shape[dim])
        up = [(i, (i + 1) % count) for i in range(count - 1)]
        down = [(j, i) for i, j in up]
        last = lax.slice_in_dim(x, length - width, length, axis=dim)
        leading = lax.slice_in_dim(x, 0, width, axis=dim)
        before = lax.ppermute(last, axis, up)
        after = lax.ppermute(leading, axis, down)
        x = jnp.concatenate([before, x, after], axis=dim)
    return x


def frame_mask(frame_count, frames):
    position = lax.broadcasted_iota(jnp.int32, (frame_count.shape[0], frames), 1)
    return (position < frame_count[:, None]).astype(jnp.float32)


def moments(values, mask, groups):
    chans, clips, frames, rows, cols = values.shape
    data = values.astype(jnp.float32).reshape(groups, chans // groups, clips, frames, rows * cols)
    first = jnp.einsum("gkbfp,bf->gb", data, mask)
    second = jnp.einsum("gkbfp,bf->gb", data * data, mask)
    return (first, second)


def normalize(values, first, second, count, gain, shift, groups):
    chans, clips, frames, rows, cols = values.shape
    mean = first / count[None, :]
    var = second / count[None, :] - mean * mean
    scale = lax.rsqrt(var + EPS)
    data = values.astype(jnp.float32).reshape(groups, chans // groups, clips, frames, rows * cols)
    normed = (data - mean[:, None, :, None, None]) * scale[:, None, :, None, None]
    normed = normed.reshape(values.shape)
    return normed * gain[:, None, None, None, None] + shift[:, None, None, None, None]


def attend(carry, queries, keys, values, scale):
    top, total, acc = carry
    scores = jnp.einsum("itc,isc->its", queries, keys, preferred_element_type=jnp.float32) * scale
    new_top = jnp.max(scores, axis=2)
    factor = jnp.exp(top - new_top)
    weights = jnp.exp(scores - new_top[..., None])
    total = total * factor + jnp.sum(weights, axis=2)
    acc = acc * factor[..., None] + jnp.einsum(
        "its,isc->itc", weights.astype(jnp.bfloat16), values, preferred_element_type=jnp.float32
    )
    return (new_top, total, acc)


def tap_stack(padded, time_tap, frames, rows, cols):
    windows = []
    for row_tap in range(3):
        for col_tap in range(3):
            windows.append(
                padded[
                    :,
                    :,
                    time_tap : time_tap + frames,
                    row_tap : row_tap + rows,
                    col_tap : col_tap + cols,
                ]
            )
    return jnp.concatenate(windows, axis=0)


def body(
    features,
    frame_count,
    norm1_gain,
    norm1_shift,
    qkv_weight,
    qkv_bias,
    out_weight,
    out_bias,
    norm2_gain,
    norm2_shift,
    conv_weight,
    conv_bias,
    cotangent,
):
    chans, clips, frames, rows, cols = features.shape
    groups = GROUPS // lax.axis_size("ch")
    mask = frame_mask(frame_count, frames)
    count = frame_count.astype(jnp.float32) * (chans // groups * rows * lax.axis_size("ha") * cols)
    first, second = moments(features, mask, groups)
    first, second = lax.psum((first, second), "ha")
    normed = normalize(features, first, second, count, norm1_gain, norm1_shift, groups).astype(
        jnp.bfloat16
    )
    by_frame = lax.all_to_all(normed, "ch", split_axis=2, concat_axis=0, tiled=True)
    width = by_frame.shape[0]
    items = clips * by_frame.shape[2]
    tok_rows = rows * cols
    tokens = by_frame.reshape(width, items, tok_rows)
    queries = lax.dot_general(
        tokens, qkv_weight[:, :width], (((0,), (0,)), ((), ())), preferred_element_type=jnp.float32
    )
    queries = (queries + qkv_bias[:width]).astype(jnp.bfloat16)
    scale = width ** (-0.5)
    start_carry = (
        jnp.full((items, tok_rows), -jnp.inf, jnp.float32),
        jnp.zeros((items, tok_rows), jnp.float32),
        jnp.zeros((items, tok_rows, width), jnp.float32),
    )
    pairs = lax.dot_general(
        tokens, qkv_weight[:, width:], (((0,), (0,)), ((), ())), preferred_element_type=jnp.float32
    )
    pairs = (pairs + qkv_bias[width:]).astype(jnp.bfloat16)
    piece = lax.all_gather(pairs, "ha", axis=1, tiled=True)
    top, total, acc = attend(start_carry, queries, piece[..., :width], piece[..., width:], scale)
    attended = (acc / total[..., None]).astype(jnp.bfloat16)
    projected = lax.dot_general(
        out_weight, attended, (((0,), (2,)), ((), ())), preferred_element_type=jnp.float32
    )
    projected = (projected + out_bias[:, None, None]).astype(jnp.bfloat16).reshape(by_frame.shape)
    update = lax.all_to_all(projected, "ch", split_axis=0, concat_axis=2, tiled=True)
    hidden = (features.astype(jnp.float32) + update.astype(jnp.float32)).astype(jnp.bfloat16)
    first, second = moments(hidden, mask, groups)
    first, second = lax.psum((first, second), "ha")
    gated = jax.nn.silu(
        normalize(hidden, first, second, count, norm2_gain, norm2_shift, groups)
    ).astype(jnp.bfloat16)
    with_rows = padded_2(gated, (("ha", 3),), 1)
    padded = jnp.pad(with_rows, ((0, 0), (0, 0), (2, 0), (0, 0), (1, 1)))
    stacks = [tap_stack(padded, time_tap, frames, rows, cols) for time_tap in range(3)]
    amount = chans * lax.axis_size("ch")
    summed = jnp.zeros((amount, clips, frames, rows, cols), jnp.float32)
    for time_tap in range(3):
        part = conv_weight[time_tap].reshape(9 * chans, amount)
        summed = summed + lax.dot_general(
            part, stacks[time_tap], (((0,), (0,)), ((), ())), preferred_element_type=jnp.float32
        )
    conv_out = lax.psum_scatter(
        summed.astype(jnp.bfloat16), "ch", scatter_dimension=0, tiled=True
    ).astype(jnp.float32)
    mixed = mask[None, :, :, None, None] * (
        hidden.astype(jnp.float32) + conv_out + conv_bias[:, None, None, None, None]
    )
    mixed = mixed.astype(jnp.bfloat16)
    masked_cot = cotangent * mask.astype(jnp.bfloat16)[None, :, :, None, None]
    full_width = chans * lax.axis_size("ch")
    carry = jnp.zeros((3, 9 * chans, full_width), jnp.float32)
    piece = lax.all_gather(masked_cot, "ch", axis=0, tiled=True)
    start = jnp.int32(0)
    for time_tap in range(3):
        part = lax.dot_general(
            stacks[time_tap],
            piece,
            (((1, 2, 3, 4), (1, 2, 3, 4)), ((), ())),
            preferred_element_type=jnp.float32,
        )
        carry = lax.dynamic_update_slice(
            carry, part[None], (jnp.int32(time_tap), jnp.int32(0), start)
        )
    grad_table = carry
    grad_table = grad_table.reshape(3, 3, 3, chans, full_width)
    weight_grad = lax.psum(grad_table, ("ha", "dp"))
    return (mixed, weight_grad)


def solution(mesh):
    placed = (
        P("ch", "dp", None, "ha", None),
        P("dp"),
        P("ch"),
        P("ch"),
        P(),
        P(),
        P(),
        P(),
        P("ch"),
        P("ch"),
        P(None, None, None, "ch", None),
        P("ch"),
        P("ch", "dp", None, "ha", None),
    )
    return jax.shard_map(
        body,
        mesh=mesh,
        in_specs=placed,
        out_specs=(P("ch", "dp", None, "ha", None), P(None, None, None, "ch", None)),
        check_vma=False,
    )
```

profile of v0, /device:TPU:0, one launch (start us, length us, event | category | flops | bytes accessed | tf_op | source)
XLA Modules:
  0.0 198.0 jit_solution(10997418595436640194)
XLA Ops:
  8.0 1.2 fusion.57
  9.2 0.1 reduce_sum.58
  9.9 0.1 reduce_sum.61
  10.0 0.1 reduce_sum.59
  10.1 0.1 reduce_sum.62
  10.2 0.1 convolution_bitcast_fusion.3
  10.3 0.1 convolution_bitcast_fusion.2
  10.4 5.9 %all-reduce.3 = (f32[8,1]{0,1:T(1,128)S(1)}, f32[8,1]{0,1:T(1,128)S(1)}) all-reduce(f32[8,1]{0,1:T(1,128)S(1)} %convolution_bitcast_fusion.3, f32[8,1]{0,1:T(1,128)S(1)} %convolution_bitcast_fusion.2), channel_id=1, replica_groups=mesh['ch'=4,'ha'=2,'dp'=4] {'ha'}, use_global_device_ids=true, to_apply=%region_2.0 | all-reduce | flops 16 | bytes 128 | tf_op jit(solution)/shard_map/psum | solution.py:96
  16.4 0.1 mul.117
  16.5 0.1 sub.66
  16.6 1.8 fusion.78
  18.4 5.5 %all-to-all-start = ((bf16[96,1,4,2,128]{4,0,3,1,2:T(8,128)(2,1)}), bf16[96,1,4,2,128]{4,0,3,1,2:T(8,128)(2,1)S(1)}, u32[]{:S(2)}, u32[]{:S(2)}) async-start(bf16[96,1,4,2,128]{4,0,3,1,2:T(8,128)(2,1)} %fusion.78), calls=%async_computation | async-start | bytes 393216 | tf_op jit(solution)/shard_map/all_to_all | solution.py:100
  24.0 0.7 slice.120
  24.7 5.5 %all-to-all-done = bf16[96,1,4,2,128]{4,0,3,1,2:T(8,128)(2,1)S(1)} async-done(((bf16[96,1,4,2,128]{4,0,3,1,2:T(8,128)(2,1)}), bf16[96,1,4,2,128]{4,0,3,1,2:T(8,128)(2,1)S(1)}, u32[]{:S(2)}, u32[]{:S(2)}) %all-to-all-start) | async-done | bytes 196640 | tf_op jit(solution)/shard_map/all_to_all | solution.py:100
  30.2 0.2 copy.32
  30.4 1.5 fusion.37
  31.8 8.9 %all-gather = bf16[512,768]{1,0:T(8,128)(2,1)S(1)} all-gather(bf16[256,768]{1,0:T(8,128)(2,1)S(1)} %fusion.37), channel_id=2, replica_groups=mesh['ch'=4,'ha'=2,'dp'=4] {'ha'}, dimensions={0}, use_global_device_ids=true | all-gather | bytes 1179648 | tf_op jit(solution)/shard_map/all_gather | solution.py:119
  40.8 1.6 fusion.104
  42.4 0.2 fusion.51
  42.7 0.6 fusion.46
  43.3 0.2 copy.33
  43.5 10.0 %all_to_all.24 = bf16[384,1,1,2,128]{4,3,2,1,0:T(2,128)(2,1)S(1)} all-to-all(bf16[384,1,1,2,128]{4,3,2,1,0:T(2,128)(2,1)S(1)} %copy.33), channel_id=1, replica_groups=mesh['ch'=4,'ha'=2,'dp'=4] {'ch'}, dimensions={0} | all-to-all | bytes 393216 | tf_op jit(solution)/shard_map/all_to_all | solution.py:126
  53.5 0.2 fusion.68
  53.7 0.1 reduce_sum.81
  53.8 0.1 reduce_sum.82
  53.9 0.1 reduce_sum.84
  54.0 0.1 reduce_sum.85
  54.1 0.1 convolution_bitcast_fusion.1
  54.2 0.1 convolution_bitcast_fusion
  54.3 5.0 %all-reduce.2 = (f32[8,1]{0,1:T(1,128)S(1)}, f32[8,1]{0,1:T(1,128)S(1)}) all-reduce(f32[8,1]{0,1:T(1,128)S(1)} %convolution_bitcast_fusion.1, f32[8,1]{0,1:T(1,128)S(1)} %convolution_bitcast_fusion), channel_id=1, replica_groups=mesh['ch'=4,'ha'=2,'dp'=4] {'ha'}, use_global_device_ids=true, to_apply=%region_10.11 | all-reduce | flops 16 | bytes 128 | tf_op jit(solution)/shard_map/psum | solution.py:129
  59.3 0.1 mul.129
  59.5 0.1 sub.75
  59.6 0.3 fusion.67
  60.0 1.3 collective-permute-start.1
  61.3 4.6 %collective-permute-start = (bf16[96,1,4,1,128]{4,0,3,2,1:T(8,128)(2,1)S(1)}, bf16[96,1,4,1,128]{4,0,3,2,1:T(8,128)(2,1)S(1)}, u32[]{:S(2)}, u32[]{:S(2)}) collective-permute-start(bf16[96,1,4,1,128]{4,0,3,2,1:T(8,128)(2,1)S(1)} %get-tuple-element.47), channel_id=1, source_target_pairs={{0,4},{1,5},{2,6},{3,7},{8,12},{9,13},{10,14},{11,15},{16,20},{17,... | collective-permute-start | bytes 294920 | tf_op jit(solution)/shard_map/ppermute | solution.py:17
  65.8 0.2 fusion.102
  66.0 0.4 collective-permute-done.1
  66.5 1.5 collective-permute-done
  68.0 0.4 fusion.41
  68.5 0.2 slice_dynamic-update-slice_fusion.13
  68.7 0.2 slice_dynamic-update-slice_fusion.12
  68.9 0.1 slice_dynamic-update-slice_fusion.11
  69.0 0.2 slice_dynamic-update-slice_fusion.10
  69.3 0.3 slice_dynamic-update-slice_fusion.9
  69.6 0.1 slice_dynamic-update-slice_fusion.8
  69.8 0.4 constant_dynamic-update-slice_fusion
  70.2 0.3 slice_dynamic-update-slice_fusion.7
  70.5 0.3 slice_dynamic-update-slice_fusion.6
  70.9 0.1 slice_dynamic-update-slice_fusion
  71.0 1.0 fusion.15
  72.1 0.6 copy-done.4
  72.6 1.0 fusion.11
  73.7 1.9 fusion.34
  75.7 0.1 copy_multiply_fusion
  75.8 21.4 %all_gather.7 = bf16[384,1,4,2,128]{4,0,3,2,1:T(8,128)(2,1)S(1)} all-gather(bf16[96,1,4,2,128]{4,0,3,2,1:T(8,128)(2,1)S(1)} %copy_multiply_fusion), channel_id=1, replica_groups=mesh['ch'=4,'ha'=2,'dp'=4] {'ch'}, dimensions={0}, use_global_device_ids=true | all-gather | bytes 983040 | tf_op jit(solution)/shard_map/all_gather | solution.py:153
  97.2 2.6 %fusion.19 = f32[1,864,384]{2,1,0:T(8,128)S(1)} fusion(bf16[864,1,4,2,128]{4,0,3,2,1:T(8,128)(2,1)} %copy-done.6, bf16[384,1,4,2,128]{4,0,3,2,1:T(8,128)(2,1)S(1)} %all_gather.7), kind=kOutput, calls=%fused_computation.21 | convolution fusion | flops 679477248 | bytes 3883008 | tf_op jit(solution)/shard_map/dot_general | solution.py:156
  99.8 2.2 %dynamic_update_slice.9 = f32[3,864,384]{2,1,0:T(8,128)} pad(f32[1,864,384]{2,1,0:T(8,128)S(1)} %fusion.19, f32[]{:T(128)} %constant.11.clone.1), padding=0_2x0_0x0_0 | pad | bytes 5308420 | tf_op jit(solution)/shard_map/dynamic_update_slice | solution.py:162
  102.0 2.2 %fusion.25 = f32[3,864,384]{2,1,0:T(8,128)} fusion(f32[3,864,384]{2,1,0:T(8,128)} %dynamic_update_slice.9, bf16[864,1,4,2,128]{4,0,3,2,1:T(8,128)(2,1)S(1)} %copy-done.5, bf16[384,1,4,2,128]{4,0,3,2,1:T(8,128)(2,1)S(1)} %all_gather.7), kind=kOutput, calls=%fused_computation.23 | convolution fusion | flops 679477248 | bytes 3883008 | tf_op jit(solution)/shard_map/dot_general | solution.py:156
  104.1 2.2 %fusion.31 = f32[3,864,384]{2,1,0:T(8,128)} fusion(f32[3,864,384]{2,1,0:T(8,128)} %fusion.25, bf16[864,1,4,2,128]{4,0,3,2,1:T(8,128)(2,1)S(1)} %slice_dynamic-update-slice_fusion, bf16[384,1,4,2,128]{4,0,3,2,1:T(8,128)(2,1)S(1)} %all_gather.7), kind=kOutput, calls=%fused_computation.25 | convolution fusion | flops 679477248 | bytes 3883008 | tf_op jit(solution)/shard_map/dot_general | solution.py:156
  106.4 0.6 copy-done.9
  107.0 1.1 fusion.71
  108.0 0.8 copy.40
  108.8 77.4 %all-reduce.6.cloned.1.call-done = f32[3,3,3,96,384]{4,3,2,1,0:T(8,128)} async-done(((f32[3,3,3,96,384]{4,3,2,1,0:T(8,128)}), f32[3,3,3,96,384]{4,3,2,1,0:T(8,128)}) %all-reduce.6.cloned.1.call-update) | async-done | bytes 3981328 | tf_op jit(solution)/shard_map/psum | solution.py:167
  186.3 4.3 %copy.98 = f32[3,3,3,96,384]{4,3,2,1,0:T(8,128)} copy(f32[3,3,3,96,384]{4,3,2,1,0:T(8,128)} %all-reduce.6.cloned.1.call-done) | data formatting | bytes 7962624
  (41 shorter events, 0.7 us)
Async XLA Ops:
  8.0 34.6 %copy-start = (bf16[384,384]{1,0:T(8,128)(2,1)S(1)}, bf16[384,384]{1,0:T(8,128)(2,1)}, u32[]{:S(2)}) copy-start(bf16[384,384]{1,0:T(8,128)(2,1)} %param.19) | copy-start | bytes 884740
  18.4 22.4 %slice-start = ((f32[1152]{0:T(1024)}), f32[384]{0:T(512)S(1)}, s32[]{:S(2)}) async-start(f32[1152]{0:T(1024)} %param.18), calls=%async_computation.5 | async-start | bytes 4096 | tf_op jit(solution)/shard_map/slice | solution.py:108
  18.4 11.8 %all-to-all-start = ((bf16[96,1,4,2,128]{4,0,3,1,2:T(8,128)(2,1)}), bf16[96,1,4,2,128]{4,0,3,1,2:T(8,128)(2,1)S(1)}, u32[]{:S(2)}, u32[]{:S(2)}) async-start(bf16[96,1,4,2,128]{4,0,3,1,2:T(8,128)(2,1)} %fusion.78), calls=%async_computation | async-start | bytes 393216 | tf_op jit(solution)/shard_map/all_to_all | solution.py:100
  24.0 82.4 %reduce-scatter.2.cloned.1.call-start = ((), (), s32[]{:S(2)}) async-start(), calls=%async_computation.3 | async-start | bytes 983040 | tf_op jit(solution)/shard_map/reduce_scatter | solution.py:143
  31.8 10.8 %copy-start.10 = (f32[384]{0:T(512)S(1)}, f32[384]{0:T(512)}, u32[]{:S(2)}) copy-start(f32[384]{0:T(512)} %param.20) | copy-start | bytes 4612
  42.6 10.8 %copy-start.2 = (bf16[96,1,4,2,128]{4,3,2,1,0:T(2,128)(2,1)S(1)}, bf16[96,1,4,2,128]{4,3,2,1,0:T(2,128)(2,1)}, u32[]{:S(2)}) copy-start(bf16[96,1,4,2,128]{4,3,2,1,0:T(2,128)(2,1)} %param.13) | copy-start | bytes 589828
  42.7 16.9 %copy-start.7 = (f32[96]{0:T(128)S(1)}, f32[96]{0:T(128)}, u32[]{:S(2)}) copy-start(f32[96]{0:T(128)} %param.22) | copy-start | bytes 1156
  42.7 16.9 %copy-start.8 = (f32[96]{0:T(128)S(1)}, f32[96]{0:T(128)}, u32[]{:S(2)}) copy-start(f32[96]{0:T(128)} %param.21) | copy-start | bytes 1156
  43.3 22.6 %copy-start.1 = (bf16[3,3,3,96,384]{4,3,2,1,0:T(8,128)(2,1)S(1)}, bf16[3,3,3,96,384]{4,3,2,1,0:T(8,128)(2,1)}, u32[]{:S(2)}) copy-start(bf16[3,3,3,96,384]{4,3,2,1,0:T(8,128)(2,1)} %param.23) | copy-start | bytes 5971972
  60.0 6.5 %collective-permute-start.1 = (bf16[96,1,4,1,128]{4,0,3,2,1:T(8,128)(2,1)S(1)}, bf16[96,1,4,1,128]{4,0,3,2,1:T(8,128)(2,1)S(1)}, u32[]{:S(2)}, u32[]{:S(2)}) collective-permute-start(bf16[96,1,4,1,128]{4,0,3,2,1:T(8,128)(2,1)S(1)} %get-tuple-element.48), channel_id=1, source_target_pairs={{4,0},{5,1},{6,2},{7,3},{12,8},{13,9},{14,10},{15,11},{20,16},{21,... | collective-permute-start | bytes 294920 | tf_op jit(solution)/shard_map/ppermute | solution.py:18
  61.3 6.8 %collective-permute-start = (bf16[96,1,4,1,128]{4,0,3,2,1:T(8,128)(2,1)S(1)}, bf16[96,1,4,1,128]{4,0,3,2,1:T(8,128)(2,1)S(1)}, u32[]{:S(2)}, u32[]{:S(2)}) collective-permute-start(bf16[96,1,4,1,128]{4,0,3,2,1:T(8,128)(2,1)S(1)} %get-tuple-element.47), channel_id=1, source_target_pairs={{0,4},{1,5},{2,6},{3,7},{8,12},{9,13},{10,14},{11,15},{16,20},{17,... | collective-permute-start | bytes 294920 | tf_op jit(solution)/shard_map/ppermute | solution.py:17
  70.8 1.2 copy-start.6
  70.8 1.8 copy-start.4
  73.7 2.0 %copy-start.3 = (bf16[96,1,4,2,128]{4,3,2,1,0:T(2,128)(2,1)S(1)}, bf16[96,1,4,2,128]{4,3,2,1,0:T(2,128)(2,1)}, u32[]{:S(2)}) copy-start(bf16[96,1,4,2,128]{4,3,2,1,0:T(2,128)(2,1)} %param.25) | copy-start | bytes 589828
  75.6 110.7 %all-reduce.6.cloned.1.call-start = ((), (), s32[]{:S(2)}) async-start(), calls=%async_computation.4 | async-start | bytes 7962624 | tf_op jit(solution)/shard_map/psum | solution.py:167
  99.8 2.2 %copy-start.5 = (bf16[864,1,4,2,128]{4,0,3,2,1:T(8,128)(2,1)S(1)}, bf16[864,1,4,2,128]{4,0,3,2,1:T(8,128)(2,1)}, u32[]{:S(2)}) copy-start(bf16[864,1,4,2,128]{4,0,3,2,1:T(8,128)(2,1)} %copy-done.4) | copy-start | bytes 5308420
  106.3 0.7 copy-start.9
Sparse Core Ops, SparseCore 0:
  75.7 27.0 reduce-scatter.1
Sparse Core Ops, SparseCore 1:
  106.4 79.8 all-reduce.5
where the time goes:
time: 199 us; the launch traced here: 198 us
  waiting for transfers between devices  85 us (43%)
  blocking collectives  51.1 us (26%)
  between operations  16.5 us (8%)
  matrix products  15 us (8%)
  local copies, waits for them, and re-layouts  12.8 us (6%)
  starting transfers between devices  11.4 us (6%)
  other arithmetic  6.16 us (3%)
    psum x1, waiting for transfers between devices, body(): weight_grad = lax.psum(grad_table, ('ha', 'dp'))  77.4 us
    all_gather x1, blocking collectives, body(): piece = lax.all_gather(masked_cot, 'ch', axis=0, tiled=True)  21.4 us
    psum x2, blocking collectives, body(): first, second = lax.psum((first, second), 'ha')  10.8 us
    all_to_all x1, blocking collectives, body(): lax.all_to_all(projected, 'ch', split_axis=0, concat_axis=2, tiled=True)  9.99 us
    all_gather x1, blocking collectives, body(): piece = lax.all_gather(pairs, 'ha', axis=1, tiled=True)  8.94 us
    unnamed x32, local copies, waits for them, and re-layouts  8.01 us
    dot_general x3, matrix products, body(): lax.dot_general(stacks[time_tap], piece, (((1, 2, 3, 4), (1, 2, 3, 4)), (...  6.9 us
    all_to_all x1, waiting for transfers between devices, body(): lax.all_to_all(normed, 'ch', split_axis=2, concat_axis=0, tiled=True)  5.55 us
  transfers between devices with their start and end apart: 5, of which 4 were waited for; matrix products, arithmetic and copies ran while one was open for 6% of the time, Pallas kernels for 0%

commit v1 on v0

--- a/solution.py
+++ b/solution.py
@@ -150,7 +150,21 @@
     masked_cot = cotangent * mask.astype(jnp.bfloat16)[None, :, :, None, None]
     full_width = chans * lax.axis_size("ch")
     carry = jnp.zeros((3, 9 * chans, full_width), jnp.float32)
-    piece = lax.all_gather(masked_cot, "ch", axis=0, tiled=True)
+    ways, here, step = (lax.axis_size("ch"), lax.axis_index("ch"), masked_cot.shape[0])
+    shape = [n * ways if d == 0 else n for d, n in enumerate(masked_cot.shape)]
+    full = lax.dynamic_update_slice_in_dim(
+        jnp.zeros(shape, masked_cot.dtype), masked_cot, here * step, axis=0
+    )
+    going_up = going_down = masked_cot
+    for far in range(1, ways // 2 + 1):
+        going_up = lax.ppermute(going_up, "ch", [(d, (d + 1) % ways) for d in range(ways)])
+        full = lax.dynamic_update_slice_in_dim(full, going_up, (here - far) % ways * step, axis=0)
+        if 2 * far < ways:
+            going_down = lax.ppermute(going_down, "ch", [(d, (d - 1) % ways) for d in range(ways)])
+            full = lax.dynamic_update_slice_in_dim(
+                full, going_down, (here + far) % ways * step, axis=0
+            )
+    piece = full
     start = jnp.int32(0)
     for time_tap in range(3):
         part = lax.dot_general(

time: 199 us -> 187 us (0.940)
  blocking collectives: 51.1 us -> 19.2 us
  starting transfers between devices: 11.4 us -> 20.2 us
  local copies, waits for them, and re-layouts: 12.8 us -> 20.3 us
  other arithmetic: 6.16 us -> 8.21 us
    all_gather x1 -> x0, blocking collectives: 21.4 us -> none  [body(): piece = lax.all_gather(masked_cot, 'ch', axis=0, tiled=True)]
    all_to_all x1 -> x0, blocking collectives: 9.99 us -> none  [body(): lax.all_to_all(projected, 'ch', split_axis=0, concat_axis=2, tiled=True)]
    psum x1, waiting for transfers between devices: 77.4 us -> 69.3 us  [body(): weight_grad = lax.psum(grad_table, ('ha', 'dp'))]
    reduce_scatter x1, waiting for transfers between devices: 0.02 us -> 6.8 us  [body(): lax.psum_scatter(summed.astype(jnp.bfloat16), 'ch', scatter_dimension=0,...]
    ppermute x0 -> x3, starting transfers between devices: none -> 5.33 us  [the longest x2 3.53 us: body(): lax.ppermute(going_up, 'ch', [(d, (d + 1) % ways) for d in range(ways)])]
    dynamic_update_slice x0 -> x4, local copies, waits for them, and re-layouts: none -> 4.77 us  [the longest x2 2.39 us: body(): lax.dynamic_update_slice_in_dim(full, going_up, (here - far) % ways * ste...]
    all_to_all x0 -> x1, waiting for transfers between devices: none -> 4.58 us  [body(): lax.all_to_all(projected, 'ch', split_axis=0, concat_axis=2, tiled=True)]
    all_to_all x0 -> x1, starting transfers between devices: none -> 3.37 us  [body(): lax.all_to_all(projected, 'ch', split_axis=0, concat_axis=2, tiled=True)]
  transfers between devices with their start and end apart: 5 -> 9, of which waited for: 4 -> 4; matrix products, arithmetic and copies ran while one was open for 6% -> 19% of each run, Pallas kernels for 0% -> 0%
where the time goes in v1:
time: 187 us; the launch traced here: 186 us
  waiting for transfers between devices  85 us (45%)
  local copies, waits for them, and re-layouts  20.3 us (11%)
  starting transfers between devices  20.2 us (11%)
  blocking collectives  19.2 us (10%)
  matrix products  16.7 us (9%)
  between operations  16.5 us (9%)
  other arithmetic  8.21 us (4%)
    psum x1, waiting for transfers between devices, body(): weight_grad = lax.psum(grad_table, ('ha', 'dp'))  69.3 us
    psum x2, blocking collectives, body(): first, second = lax.psum((first, second), 'ha')  10.8 us
    dot_general x3, matrix products, body(): lax.dot_general(stacks[time_tap], piece, (((1, 2, 3, 4), (1, 2, 3, 4)), (...  9.48 us
    all_gather x1, blocking collectives, body(): piece = lax.all_gather(pairs, 'ha', axis=1, tiled=True)  8.45 us
    unnamed x40, local copies, waits for them, and re-layouts  8.01 us
    reduce_scatter x1, waiting for transfers between devices, body(): lax.psum_scatter(summed.astype(jnp.bfloat16), 'ch', scatter_dimension=0,...  6.8 us
    all_to_all x1, starting transfers between devices, body(): lax.all_to_all(normed, 'ch', split_axis=2, concat_axis=0, tiled=True)  5.41 us
    all_to_all x1, waiting for transfers between devices, body(): lax.all_to_all(projected, 'ch', split_axis=0, concat_axis=2, tiled=True)  4.58 us
  transfers between devices with their start and end apart: 9, of which 4 were waited for; matrix products, arithmetic and copies ran while one was open for 19% of the time, Pallas kernels for 0%

profile of v1, /device:TPU:0, one launch (start us, length us, event | category | flops | bytes accessed | tf_op | source)
XLA Modules:
  0.0 186.3 jit_solution(9749135152053624939)
XLA Ops:
  8.0 1.2 fusion.54
  10.1 0.1 reduce_sum.59
  10.3 0.1 convolution_bitcast_fusion.3
  10.4 0.1 convolution_bitcast_fusion.2
  10.5 5.9 %all-reduce.3 = (f32[8,1]{0,1:T(1,128)S(1)}, f32[8,1]{0,1:T(1,128)S(1)}) all-reduce(f32[8,1]{0,1:T(1,128)S(1)} %convolution_bitcast_fusion.3, f32[8,1]{0,1:T(1,128)S(1)} %convolution_bitcast_fusion.2), channel_id=1, replica_groups=mesh['ch'=4,'ha'=2,'dp'=4] {'ha'}, use_global_device_ids=true, to_apply=%region_2.0 | all-reduce | flops 16 | bytes 128 | tf_op jit(solution)/shard_map/psum | solution.py:96
  16.7 1.8 fusion.75
  18.5 5.4 %all-to-all-start = ((bf16[96,1,4,2,128]{4,0,3,1,2:T(8,128)(2,1)}), bf16[96,1,4,2,128]{4,0,3,1,2:T(8,128)(2,1)S(1)}, u32[]{:S(2)}, u32[]{:S(2)}) async-start(bf16[96,1,4,2,128]{4,0,3,1,2:T(8,128)(2,1)} %fusion.75), calls=%async_computation | async-start | bytes 393216 | tf_op jit(solution)/shard_map/all_to_all | solution.py:100
  23.9 1.9 %broadcast_multiply_fusion = bf16[96,1,4,2,128]{4,3,2,1,0:T(2,128)(2,1)} fusion(bf16[96,1,4,2,128]{4,3,2,1,0:T(2,128)(2,1)} %param.25, bf16[4]{0:T(256)(128)(2,1)S(1)} %fusion.96), kind=kLoop, calls=%fused_computation.121 | loop fusion | flops 98304 | bytes 393224 | tf_op jit(solution)/shard_map/mul | solution.py:150
  25.8 2.0 %collective-permute-start.2 = (bf16[96,1,4,2,128]{4,3,2,1,0:T(2,128)(2,1)}, bf16[96,1,4,2,128]{4,3,2,1,0:T(2,128)(2,1)}, u32[]{:S(2)}, u32[]{:S(2)}) collective-permute-start(bf16[96,1,4,2,128]{4,3,2,1,0:T(2,128)(2,1)} %broadcast_multiply_fusion), channel_id=1, source_target_pairs={{0,8},{8,16},{16,24},{24,0},{1,9},{9,17},{17,25},{25,1},{2,10},{10... | collective-permute-start | bytes 589832 | tf_op jit(solution)/shard_map/ppermute | solution.py:160
  27.8 1.8 collective-permute-start.3
  29.6 0.7 slice.120
  30.3 4.3 %all-to-all-done = bf16[96,1,4,2,128]{4,0,3,1,2:T(8,128)(2,1)S(1)} async-done(((bf16[96,1,4,2,128]{4,0,3,1,2:T(8,128)(2,1)}), bf16[96,1,4,2,128]{4,0,3,1,2:T(8,128)(2,1)S(1)}, u32[]{:S(2)}, u32[]{:S(2)}) %all-to-all-start) | async-done | bytes 196640 | tf_op jit(solution)/shard_map/all_to_all | solution.py:100
  34.6 0.2 copy.38
  34.8 0.4 fusion.37
  35.2 8.4 %all-gather = bf16[512,768]{1,0:T(8,128)(2,1)S(1)} all-gather(bf16[256,768]{1,0:T(8,128)(2,1)S(1)} %fusion.37), channel_id=2, replica_groups=mesh['ch'=4,'ha'=2,'dp'=4] {'ha'}, dimensions={0}, use_global_device_ids=true | all-gather | bytes 1179648 | tf_op jit(solution)/shard_map/all_gather | solution.py:119
  43.6 0.6 fusion.101
  44.3 0.2 fusion.48
  44.5 0.6 copy-done.6
  45.1 1.8 fusion.46
  46.9 0.9 copy.39
  47.7 3.4 %all-to-all-start.1 = ((bf16[384,1,1,2,128]{4,3,2,1,0:T(2,128)(2,1)}), bf16[384,1,1,2,128]{4,3,2,1,0:T(2,128)(2,1)S(1)}, u32[]{:S(2)}, u32[]{:S(2)}) async-start(bf16[384,1,1,2,128]{4,3,2,1,0:T(2,128)(2,1)} %copy.39), calls=%async_computation.1 | async-start | bytes 393216 | tf_op jit(solution)/shard_map/all_to_all | solution.py:126
  51.2 0.2 fusion.117
  51.5 1.3 fusion.99
  52.7 4.6 %all-to-all-done.1 = bf16[384,1,1,2,128]{4,3,2,1,0:T(2,128)(2,1)S(1)} async-done(((bf16[384,1,1,2,128]{4,3,2,1,0:T(2,128)(2,1)}), bf16[384,1,1,2,128]{4,3,2,1,0:T(2,128)(2,1)S(1)}, u32[]{:S(2)}, u32[]{:S(2)}) %all-to-all-start.1) | async-done | bytes 196640 | tf_op jit(solution)/shard_map/all_to_all | solution.py:126
  57.4 0.2 fusion.65
  57.7 0.1 reduce_sum.82
  57.8 0.1 reduce_sum.85
  57.9 0.1 convolution_bitcast_fusion.1
  58.0 0.1 convolution_bitcast_fusion
  58.2 4.9 %all-reduce.2 = (f32[8,1]{0,1:T(1,128)S(1)}, f32[8,1]{0,1:T(1,128)S(1)}) all-reduce(f32[8,1]{0,1:T(1,128)S(1)} %convolution_bitcast_fusion.1, f32[8,1]{0,1:T(1,128)S(1)} %convolution_bitcast_fusion), channel_id=1, replica_groups=mesh['ch'=4,'ha'=2,'dp'=4] {'ha'}, use_global_device_ids=true, to_apply=%region_10.11 | all-reduce | flops 16 | bytes 128 | tf_op jit(solution)/shard_map/psum | solution.py:129
  63.4 0.3 fusion.64
  63.8 1.3 collective-permute-start.1
  65.1 4.6 %collective-permute-start = (bf16[96,1,4,1,128]{4,0,3,2,1:T(8,128)(2,1)S(1)}, bf16[96,1,4,1,128]{4,0,3,2,1:T(8,128)(2,1)S(1)}, u32[]{:S(2)}, u32[]{:S(2)}) collective-permute-start(bf16[96,1,4,1,128]{4,0,3,2,1:T(8,128)(2,1)S(1)} %get-tuple-element.47), channel_id=1, source_target_pairs={{0,4},{1,5},{2,6},{3,7},{8,12},{9,13},{10,14},{11,15},{16,20},{17,... | collective-permute-start | bytes 294920 | tf_op jit(solution)/shard_map/ppermute | solution.py:17
  69.7 1.0 broadcast.127
  70.6 0.7 copy_dynamic-update-slice_fusion.3
  71.3 1.5 collective-permute-start.4
  72.9 0.4 fusion.41
  73.3 0.2 slice_dynamic-update-slice_fusion.13
  73.5 0.3 slice_dynamic-update-slice_fusion.12
  73.8 0.1 slice_dynamic-update-slice_fusion.11
  73.9 0.3 slice_dynamic-update-slice_fusion.10
  74.2 0.3 slice_dynamic-update-slice_fusion.9
  74.5 0.1 slice_dynamic-update-slice_fusion.8
  74.7 0.4 constant_dynamic-update-slice_fusion
  75.1 0.3 slice_dynamic-update-slice_fusion.7
  75.4 0.3 slice_dynamic-update-slice_fusion.6
  75.8 0.1 slice_dynamic-update-slice_fusion
  75.9 1.0 fusion.15
  77.0 0.5 copy-done.7
  77.5 1.0 fusion.11
  78.6 1.9 %fusion.34 = bf16[384,1,4,2,128]{4,0,3,2,1:T(8,128)(2,1)} fusion(bf16[864,384,1,1]{1,0,3,2:T(8,128)(2,1)S(1)} %bitcast.169, bf16[864,1,4,2,128]{4,0,3,2,1:T(8,128)(2,1)S(1)} %slice_dynamic-update-slice_fusion, f32[4,2,128,384]{2,3,1,0:T(8,128)S(1)} %fusion.15, f32[4,2,128,384]{2,3,1,0:T(8,128)S(1)} %fusion.11), kind=kOutput, calls=%fused_computation.26 | convolution fusion | flops 680656896 | bytes 6365184 | tf_op jit(solution)/shard_map/dot_general | solution.py:140
  80.5 0.2 all-reduce.6.cloned.1.call-start
  80.8 1.6 copy_dynamic-update-slice_fusion.2
  82.4 1.7 copy_dynamic-update-slice_fusion.1
  84.1 0.7 copy_dynamic-update-slice_fusion
  84.8 2.9 %fusion.19 = f32[1,864,384]{2,1,0:T(8,128)S(1)} fusion(bf16[384,4,2,128]{3,0,2,1:T(8,128)(2,1)} %copy_dynamic-update-slice_fusion, bf16[864,1,4,2,128]{4,0,3,2,1:T(8,128)(2,1)} %copy-done.9), kind=kOutput, calls=%fused_computation.21 | convolution fusion | flops 679477248 | bytes 3883008 | tf_op jit(solution)/shard_map/dot_general | solution.py:170
  87.7 2.2 %dynamic_update_slice.29 = f32[3,864,384]{2,1,0:T(8,128)} pad(f32[1,864,384]{2,1,0:T(8,128)S(1)} %fusion.19, f32[]{:T(128)} %constant.47.clone.1), padding=0_2x0_0x0_0 | pad | bytes 5308420 | tf_op jit(solution)/shard_map/dynamic_update_slice | solution.py:176
  89.9 3.3 %fusion.25 = f32[3,864,384]{2,1,0:T(8,128)} fusion(f32[3,864,384]{2,1,0:T(8,128)} %dynamic_update_slice.29, bf16[384,4,2,128]{3,0,2,1:T(8,128)(2,1)} %copy_dynamic-update-slice_fusion, bf16[864,1,4,2,128]{4,0,3,2,1:T(8,128)(2,1)S(1)} %copy-done.8), kind=kOutput, calls=%fused_computation.23 | convolution fusion | flops 679477248 | bytes 3883008 | tf_op jit(solution)/shard_map/dot_general | solution.py:170
  93.2 3.3 %fusion.31 = f32[3,864,384]{2,1,0:T(8,128)} fusion(f32[3,864,384]{2,1,0:T(8,128)} %fusion.25, bf16[384,4,2,128]{3,0,2,1:T(8,128)(2,1)} %copy_dynamic-update-slice_fusion, bf16[864,1,4,2,128]{4,0,3,2,1:T(8,128)(2,1)S(1)} %slice_dynamic-update-slice_fusion), kind=kOutput, calls=%fused_computation.25 | convolution fusion | flops 679477248 | bytes 3883008 | tf_op jit(solution)/shard_map/dot_general | solution.py:170
  96.6 6.8 %reduce-scatter.2.cloned.1.call-done = bf16[96,1,4,2,128]{4,0,3,2,1:T(8,128)(2,1)} async-done(((bf16[384,1,4,2,128]{4,0,3,2,1:T(8,128)(2,1)}), bf16[96,1,4,2,128]{4,0,3,2,1:T(8,128)(2,1)}) %reduce-scatter.2.cloned.1.call-update) | async-done | bytes 196624 | tf_op jit(solution)/shard_map/reduce_scatter | solution.py:143
  103.4 1.1 fusion.68
  104.4 0.8 copy.49
  105.2 69.3 %all-reduce.6.cloned.1.call-done = f32[3,3,3,96,384]{4,3,2,1,0:T(8,128)} async-done(((f32[3,3,3,96,384]{4,3,2,1,0:T(8,128)}), f32[3,3,3,96,384]{4,3,2,1,0:T(8,128)}) %all-reduce.6.cloned.1.call-update) | async-done | bytes 3981328 | tf_op jit(solution)/shard_map/psum | solution.py:181
  174.5 4.3 %copy.114 = f32[3,3,3,96,384]{4,3,2,1,0:T(8,128)} copy(f32[3,3,3,96,384]{4,3,2,1,0:T(8,128)} %all-reduce.6.cloned.1.call-done) | data formatting | bytes 7962624
  (61 shorter events, 1.4 us)
Async XLA Ops:
  8.0 37.1 %copy-start = (bf16[384,384]{1,0:T(8,128)(2,1)S(1)}, bf16[384,384]{1,0:T(8,128)(2,1)}, u32[]{:S(2)}) copy-start(bf16[384,384]{1,0:T(8,128)(2,1)} %param.19) | copy-start | bytes 884740
  8.0 26.8 %copy-start.13 = (bf16[384,1152]{1,0:T(8,128)(2,1)S(1)}, bf16[384,1152]{1,0:T(8,128)(2,1)}, u32[]{:S(2)}) copy-start(bf16[384,1152]{1,0:T(8,128)(2,1)} %param.17) | copy-start | bytes 2654212
  18.5 16.1 %all-to-all-start = ((bf16[96,1,4,2,128]{4,0,3,1,2:T(8,128)(2,1)}), bf16[96,1,4,2,128]{4,0,3,1,2:T(8,128)(2,1)S(1)}, u32[]{:S(2)}, u32[]{:S(2)}) async-start(bf16[96,1,4,2,128]{4,0,3,1,2:T(8,128)(2,1)} %fusion.75), calls=%async_computation | async-start | bytes 393216 | tf_op jit(solution)/shard_map/all_to_all | solution.py:100
  23.9 19.7 %slice-start = ((f32[1152]{0:T(1024)}), f32[384]{0:T(512)S(1)}, s32[]{:S(2)}) async-start(f32[1152]{0:T(1024)} %param.18), calls=%async_computation.5 | async-start | bytes 4096 | tf_op jit(solution)/shard_map/slice | solution.py:108
  25.8 45.6 %collective-permute-start.2 = (bf16[96,1,4,2,128]{4,3,2,1,0:T(2,128)(2,1)}, bf16[96,1,4,2,128]{4,3,2,1,0:T(2,128)(2,1)}, u32[]{:S(2)}, u32[]{:S(2)}) collective-permute-start(bf16[96,1,4,2,128]{4,3,2,1,0:T(2,128)(2,1)} %broadcast_multiply_fusion), channel_id=1, source_target_pairs={{0,8},{8,16},{16,24},{24,0},{1,9},{9,17},{17,25},{25,1},{2,10},{10... | collective-permute-start | bytes 589832 | tf_op jit(solution)/shard_map/ppermute | solution.py:160
  27.8 54.6 %collective-permute-start.3 = (bf16[96,1,4,2,128]{4,3,2,1,0:T(2,128)(2,1)}, bf16[96,1,4,2,128]{4,3,2,1,0:T(2,128)(2,1)}, u32[]{:S(2)}, u32[]{:S(2)}) collective-permute-start(bf16[96,1,4,2,128]{4,3,2,1,0:T(2,128)(2,1)} %broadcast_multiply_fusion), channel_id=1, source_target_pairs={{0,24},{8,0},{16,8},{24,16},{1,25},{9,1},{17,9},{25,17},{2,26},{10... | collective-permute-start | bytes 589832 | tf_op jit(solution)/shard_map/ppermute | solution.py:163
  35.2 9.9 %copy-start.14 = (f32[384]{0:T(512)S(1)}, f32[384]{0:T(512)}, u32[]{:S(2)}) copy-start(f32[384]{0:T(512)} %param.20) | copy-start | bytes 4612
  44.3 0.8 copy-start.6
  45.1 6.1 %copy-start.3 = (bf16[96,1,4,2,128]{4,3,2,1,0:T(2,128)(2,1)S(1)}, bf16[96,1,4,2,128]{4,3,2,1,0:T(2,128)(2,1)}, u32[]{:S(2)}) copy-start(bf16[96,1,4,2,128]{4,3,2,1,0:T(2,128)(2,1)} %param.25) | copy-start | bytes 589828
  45.1 6.3 %copy-start.1 = (bf16[3,3,3,96,384]{4,3,2,1,0:T(8,128)(2,1)S(1)}, bf16[3,3,3,96,384]{4,3,2,1,0:T(8,128)(2,1)}, u32[]{:S(2)}) copy-start(bf16[3,3,3,96,384]{4,3,2,1,0:T(8,128)(2,1)} %param.23) | copy-start | bytes 5971972
  47.7 9.6 %all-to-all-start.1 = ((bf16[384,1,1,2,128]{4,3,2,1,0:T(2,128)(2,1)}), bf16[384,1,1,2,128]{4,3,2,1,0:T(2,128)(2,1)S(1)}, u32[]{:S(2)}, u32[]{:S(2)}) async-start(bf16[384,1,1,2,128]{4,3,2,1,0:T(2,128)(2,1)} %copy.39), calls=%async_computation.1 | async-start | bytes 393216 | tf_op jit(solution)/shard_map/all_to_all | solution.py:126
  51.1 52.3 %reduce-scatter.2.cloned.1.call-start = ((), (), s32[]{:S(2)}) async-start(), calls=%async_computation.3 | async-start | bytes 983040 | tf_op jit(solution)/shard_map/reduce_scatter | solution.py:143
  51.4 5.9 %copy-start.2 = (bf16[96,1,4,2,128]{4,3,2,1,0:T(2,128)(2,1)S(1)}, bf16[96,1,4,2,128]{4,3,2,1,0:T(2,128)(2,1)}, u32[]{:S(2)}) copy-start(bf16[96,1,4,2,128]{4,3,2,1,0:T(2,128)(2,1)} %param.13) | copy-start | bytes 589828
  51.4 12.0 %copy-start.10 = (f32[96]{0:T(128)S(1)}, f32[96]{0:T(128)}, u32[]{:S(2)}) copy-start(f32[96]{0:T(128)} %param.22) | copy-start | bytes 1156
  51.4 12.0 %copy-start.11 = (f32[96]{0:T(128)S(1)}, f32[96]{0:T(128)}, u32[]{:S(2)}) copy-start(f32[96]{0:T(128)} %param.21) | copy-start | bytes 1156
  63.8 9.1 %collective-permute-start.1 = (bf16[96,1,4,1,128]{4,0,3,2,1:T(8,128)(2,1)S(1)}, bf16[96,1,4,1,128]{4,0,3,2,1:T(8,128)(2,1)S(1)}, u32[]{:S(2)}, u32[]{:S(2)}) collective-permute-start(bf16[96,1,4,1,128]{4,0,3,2,1:T(8,128)(2,1)S(1)} %get-tuple-element.48), channel_id=1, source_target_pairs={{4,0},{5,1},{6,2},{7,3},{12,8},{13,9},{14,10},{15,11},{20,16},{21,... | collective-permute-start | bytes 294920 | tf_op jit(solution)/shard_map/ppermute | solution.py:18
  65.1 7.8 %collective-permute-start = (bf16[96,1,4,1,128]{4,0,3,2,1:T(8,128)(2,1)S(1)}, bf16[96,1,4,1,128]{4,0,3,2,1:T(8,128)(2,1)S(1)}, u32[]{:S(2)}, u32[]{:S(2)}) collective-permute-start(bf16[96,1,4,1,128]{4,0,3,2,1:T(8,128)(2,1)S(1)} %get-tuple-element.47), channel_id=1, source_target_pairs={{0,4},{1,5},{2,6},{3,7},{8,12},{9,13},{10,14},{11,15},{16,20},{17,... | collective-permute-start | bytes 294920 | tf_op jit(solution)/shard_map/ppermute | solution.py:17
  71.3 12.7 %collective-permute-start.4 = (bf16[96,1,4,2,128]{4,3,2,1,0:T(2,128)(2,1)}, bf16[96,1,4,2,128]{4,3,2,1,0:T(2,128)(2,1)S(1)}, u32[]{:S(2)}, u32[]{:S(2)}) collective-permute-start(bf16[96,1,4,2,128]{4,3,2,1,0:T(2,128)(2,1)} %collective-permute-done.2), channel_id=1, source_target_pairs={{0,8},{8,16},{16,24},{24,0},{1,9},{9,17},{17,25},{25,1},{2,10},{10... | collective-permute-start | bytes 589832 | tf_op jit(solution)/shard_map/ppermute | solution.py:160
  74.7 1.2 copy-start.5
  75.7 1.3 copy-start.9
  75.7 1.8 copy-start.7
  75.9 1.6 copy-start.4
  80.5 94.0 %all-reduce.6.cloned.1.call-start = ((), (), s32[]{:S(2)}) async-start(), calls=%async_computation.4 | async-start | bytes 7962624 | tf_op jit(solution)/shard_map/psum | solution.py:181
  87.7 2.2 %copy-start.8 = (bf16[864,1,4,2,128]{4,0,3,2,1:T(8,128)(2,1)S(1)}, bf16[864,1,4,2,128]{4,0,3,2,1:T(8,128)(2,1)}, u32[]{:S(2)}) copy-start(bf16[864,1,4,2,128]{4,0,3,2,1:T(8,128)(2,1)} %copy-done.7) | copy-start | bytes 5308420
  96.5 6.8 %copy-start.12 = (f32[96]{0:T(128)S(1)}, f32[96]{0:T(128)}, u32[]{:S(2)}) copy-start(f32[96]{0:T(128)} %param.24) | copy-start | bytes 1156
Sparse Core Ops, SparseCore 0:
  80.6 22.6 reduce-scatter.1
Sparse Core Ops, SparseCore 1:
  96.6 77.8 all-reduce.5
